TPU v7x, 32 devices: a whole 2x2x4 slice. The times are simulated.
32 devices in a mesh: pipe: 4 (over z), dp: 2 (over x), tensor: 4 (over y, core).
Axes of the slice: x: 2, y: 2, z: 4, core: 2. Of those that a mesh axis runs over, the one named last changes fastest.
Arguments:
- acts: bfloat16 [4, 4, 128, 8192], P('pipe', None, 'dp', 'tensor'), may hold values from -6 to 6
- w_in: bfloat16 [4, 8192, 512], P('pipe', 'tensor', 'dp'), may hold values from -0.0625 to 0.0625
- w_out: bfloat16 [4, 512, 8192], P('pipe', 'dp', 'tensor'), may hold values from -0.25 to 0.25
- top_grad: bfloat16 [4, 128, 8192], P(None, 'dp', 'tensor'), may hold values from -6 to 6
Outputs:
- grad_input: bfloat16 [4, 4, 128, 8192], P('pipe', None, 'dp', 'tensor')
- grad_w_in: bfloat16 [4, 8192, 512], P('pipe', 'tensor', 'dp')
- grad_w_out: bfloat16 [4, 512, 8192], P('pipe', 'dp', 'tensor')
All inputs are finite; a program needn't handle non-finite values.
Results may differ from a plain program's by a relative error of at most 0.013.
Values may be sent and summed in bfloat16 or wider, within the bound.
A program may use at most 64 MiB of HBM per device.

v0:
```python
import jax
import jax.numpy as jnp
from jax import lax
from jax.sharding import PartitionSpec as P


def shifted(shard, axis, by):
    devices = lax.axis_size(axis)
    pairs = [(i, i + by) for i in range(devices) if 0 <= i + by < devices]
    return lax.ppermute(shard, axis, pairs)


def silu_slope(value):
    sig = jax.nn.sigmoid(value)
    return sig * (1.0 + value * (1.0 - sig))


def put_slot(store, piece, slot, active):
    updated = lax.dynamic_update_index_in_dim(store, piece, slot, 0)
    return jnp.where(active, updated, store)


def shards(acts, w_in, w_out, top_grad):
    pipes = lax.axis_size("pipe")
    section = lax.axis_index("pipe")
    micro = acts.shape[1]
    rows = acts.shape[2]
    width = acts.shape[3]
    saved = acts[0]
    w_in_full, w_out_full = (
        lax.all_gather(w_in[0], "dp", axis=1, tiled=True),
        lax.all_gather(w_out[0], "dp", axis=0, tiled=True),
    )
    inner = w_in_full.shape[1]
    contract = (((1,), (1,)), ((), ()))
    incoming = jnp.zeros((rows, width), jnp.bfloat16)
    dpre_store = jnp.zeros((micro, rows, inner), jnp.bfloat16)
    act_store = jnp.zeros((micro, rows, inner), jnp.bfloat16)
    grad_store = jnp.zeros((micro, rows, width), jnp.bfloat16)
    back_store = jnp.zeros((micro, rows, width), jnp.bfloat16)
    total_steps = micro + pipes - 1
    for step in range(total_steps):
        index = step - (pipes - 1 - section)
        active = jnp.logical_and(index >= 0, index < micro)
        slot = jnp.clip(index, 0, micro - 1)
        top_piece = lax.dynamic_index_in_dim(top_grad, slot, 0, keepdims=False)
        grad_now = jnp.where(section == pipes - 1, top_piece, incoming)
        x_now = lax.dynamic_index_in_dim(saved, slot, 0, keepdims=False)
        pre_part = jnp.dot(x_now, w_in_full, preferred_element_type=jnp.float32)
        pre_now = lax.psum(pre_part, "tensor")
        hidden_part = lax.dot_general(
            grad_now, w_out_full, contract, preferred_element_type=jnp.float32
        )
        hidden = lax.psum(hidden_part, "tensor")
        dpre = (hidden * silu_slope(pre_now)).astype(jnp.bfloat16)
        branch = lax.dot_general(dpre, w_in_full, contract, preferred_element_type=jnp.float32)
        back = (grad_now.astype(jnp.float32) + branch).astype(jnp.bfloat16)
        dpre_store = put_slot(dpre_store, dpre, slot, active)
        act_store = put_slot(act_store, jax.nn.silu(pre_now).astype(jnp.bfloat16), slot, active)
        grad_store = put_slot(grad_store, grad_now, slot, active)
        back_store = put_slot(back_store, back, slot, active)
        if step + 1 < total_steps:
            incoming = shifted(back, "pipe", -1)
    token_dims = (((0,), (0,)), ((), ()))
    flat_x = saved.reshape(micro * rows, width)
    part_in = lax.dot_general(
        flat_x,
        dpre_store.reshape(micro * rows, inner),
        token_dims,
        preferred_element_type=jnp.float32,
    )
    part_out = lax.dot_general(
        act_store.reshape(micro * rows, inner),
        grad_store.reshape(micro * rows, width),
        token_dims,
        preferred_element_type=jnp.float32,
    )
    summed_in, summed_out = (
        lax.psum_scatter(
            part_in.astype(jnp.bfloat16), "dp", scatter_dimension=1, tiled=True
        ).astype(jnp.float32),
        lax.psum_scatter(
            part_out.astype(jnp.bfloat16), "dp", scatter_dimension=0, tiled=True
        ).astype(jnp.float32),
    )
    return (
        back_store[None],
        summed_in.astype(jnp.bfloat16)[None],
        summed_out.astype(jnp.bfloat16)[None],
    )


def solution(mesh):
    placed = (
        P("pipe", None, "dp", "tensor"),
        P("pipe", "tensor", "dp"),
        P("pipe", "dp", "tensor"),
        P(None, "dp", "tensor"),
    )
    return jax.shard_map(
        shards,
        mesh=mesh,
        in_specs=placed,
        out_specs=(
            P("pipe", None, "dp", "tensor"),
            P("pipe", "tensor", "dp"),
            P("pipe", "dp", "tensor"),
        ),
        check_vma=False,
    )
```

profile of v0, /device:TPU:0, one launch (start us, length us, event | category | flops | bytes accessed | tf_op | source)
XLA Modules:
  0.0 486.9 jit_solution(4687135771134606875)
XLA Ops:
  8.7 36.6 %all-gather.7.cloned.1.call-done = bf16[1,2048,512]{2,1,0:T(8,128)(2,1)} async-done(((bf16[1,2048,256]{2,1,0:T(8,128)(2,1)}), bf16[1,2048,512]{2,1,0:T(8,128)(2,1)}) %all-gather.7.cloned.1.call-update) | async-done | bytes 2097168 | tf_op jit(solution)/shard_map/all_gather | solution.py:31
  45.4 2.7 fusion.27
  48.1 32.0 %all-gather.5.cloned.1.call-done = bf16[1,512,2048]{2,1,0:T(8,128)(2,1)} async-done(((bf16[1,256,2048]{2,1,0:T(8,128)(2,1)}), bf16[1,512,2048]{2,1,0:T(8,128)(2,1)}) %all-gather.5.cloned.1.call-update) | async-done | bytes 2097168 | tf_op jit(solution)/shard_map/all_gather | solution.py:32
  80.1 3.1 fusion.41
  84.3 1.7 select_dynamic-update-slice_fusion
  86.0 29.4 %all-reduce.27.cloned.1.call-done = (f32[64,512]{1,0:T(8,128)}, f32[64,512]{1,0:T(8,128)}) async-done(((f32[64,512]{1,0:T(8,128)}, f32[64,512]{1,0:T(8,128)}), (f32[64,512]{1,0:T(8,128)}, f32[64,512]{1,0:T(8,128)})) %all-reduce.27.cloned.1.call-update) | async-done | bytes 262160 | tf_op jit(solution)/shard_map/psum | solution.py:54
  117.6 2.4 bitcast_dynamic-update-slice_fusion
  120.0 1.4 collective-permute-start
  122.6 6.3 %collective-permute-done = bf16[64,2048]{1,0:T(8,128)(2,1)S(1)} collective-permute-done((bf16[64,2048]{1,0:T(8,128)(2,1)S(1)}, bf16[64,2048]{1,0:T(8,128)(2,1)S(1)}, u32[]{:S(2)}, u32[]{:S(2)}) %collective-permute-start) | collective-permute-done | bytes 262176 | tf_op jit(solution)/shard_map/ppermute | solution.py:10
  128.8 1.8 fusion.52
  134.3 30.6 %all-reduce.25.cloned.1.call-done = (f32[64,512]{1,0:T(8,128)}, f32[64,512]{1,0:T(8,128)}) async-done(((f32[64,512]{1,0:T(8,128)}, f32[64,512]{1,0:T(8,128)}), (f32[64,512]{1,0:T(8,128)}, f32[64,512]{1,0:T(8,128)})) %all-reduce.25.cloned.1.call-update) | async-done | bytes 262160 | tf_op jit(solution)/shard_map/psum | solution.py:54
  164.9 1.7 fusion.85
  166.5 2.5 fusion.62
  171.6 6.3 %collective-permute-done.1 = bf16[64,2048]{1,0:T(8,128)(2,1)S(1)} collective-permute-done((bf16[64,2048]{1,0:T(8,128)(2,1)S(1)}, bf16[64,2048]{1,0:T(8,128)(2,1)S(1)}, u32[]{:S(2)}, u32[]{:S(2)}) %collective-permute-start.1) | collective-permute-done | bytes 262176 | tf_op jit(solution)/shard_map/ppermute | solution.py:10
  177.8 1.8 fusion.51
  181.9 32.0 %all-reduce.23.cloned.1.call-done = (f32[64,512]{1,0:T(8,128)}, f32[64,512]{1,0:T(8,128)}) async-done(((f32[64,512]{1,0:T(8,128)}, f32[64,512]{1,0:T(8,128)}), (f32[64,512]{1,0:T(8,128)}, f32[64,512]{1,0:T(8,128)})) %all-reduce.23.cloned.1.call-update) | async-done | bytes 262160 | tf_op jit(solution)/shard_map/psum | solution.py:54
  213.8 1.7 fusion.84
  215.5 2.5 fusion.60
  218.0 1.4 collective-permute-start.2
  220.5 6.3 %collective-permute-done.2 = bf16[64,2048]{1,0:T(8,128)(2,1)S(1)} collective-permute-done((bf16[64,2048]{1,0:T(8,128)(2,1)S(1)}, bf16[64,2048]{1,0:T(8,128)(2,1)S(1)}, u32[]{:S(2)}, u32[]{:S(2)}) %collective-permute-start.2) | collective-permute-done | bytes 262176 | tf_op jit(solution)/shard_map/ppermute | solution.py:10
  226.8 1.8 fusion.50
  230.9 32.0 %all-reduce.21.cloned.1.call-done = (f32[64,512]{1,0:T(8,128)}, f32[64,512]{1,0:T(8,128)}) async-done(((f32[64,512]{1,0:T(8,128)}, f32[64,512]{1,0:T(8,128)}), (f32[64,512]{1,0:T(8,128)}, f32[64,512]{1,0:T(8,128)})) %all-reduce.21.cloned.1.call-update) | async-done | bytes 262160 | tf_op jit(solution)/shard_map/psum | solution.py:54
  262.8 1.7 fusion.83
  264.5 2.5 fusion.58
  267.0 1.4 collective-permute-start.3
  269.6 6.3 %collective-permute-done.3 = bf16[64,2048]{1,0:T(8,128)(2,1)S(1)} collective-permute-done((bf16[64,2048]{1,0:T(8,128)(2,1)S(1)}, bf16[64,2048]{1,0:T(8,128)(2,1)S(1)}, u32[]{:S(2)}, u32[]{:S(2)}) %collective-permute-start.3) | collective-permute-done | bytes 262176 | tf_op jit(solution)/shard_map/ppermute | solution.py:10
  275.8 1.8 fusion.49
  279.9 32.0 %all-reduce.19.cloned.1.call-done = (f32[64,512]{1,0:T(8,128)}, f32[64,512]{1,0:T(8,128)}) async-done(((f32[64,512]{1,0:T(8,128)}, f32[64,512]{1,0:T(8,128)}), (f32[64,512]{1,0:T(8,128)}, f32[64,512]{1,0:T(8,128)})) %all-reduce.19.cloned.1.call-update) | async-done | bytes 262160 | tf_op jit(solution)/shard_map/psum | solution.py:54
  311.8 1.7 fusion.82
  313.5 2.5 fusion.56
  316.0 1.4 collective-permute-start.4
  318.5 6.3 %collective-permute-done.4 = bf16[64,2048]{1,0:T(8,128)(2,1)S(1)} collective-permute-done((bf16[64,2048]{1,0:T(8,128)(2,1)S(1)}, bf16[64,2048]{1,0:T(8,128)(2,1)S(1)}, u32[]{:S(2)}, u32[]{:S(2)}) %collective-permute-start.4) | collective-permute-done | bytes 262176 | tf_op jit(solution)/shard_map/ppermute | solution.py:10
  324.8 1.8 fusion.48
  328.9 32.0 %all-reduce.17.cloned.1.call-done = (f32[64,512]{1,0:T(8,128)}, f32[64,512]{1,0:T(8,128)}) async-done(((f32[64,512]{1,0:T(8,128)}, f32[64,512]{1,0:T(8,128)}), (f32[64,512]{1,0:T(8,128)}, f32[64,512]{1,0:T(8,128)})) %all-reduce.17.cloned.1.call-update) | async-done | bytes 262160 | tf_op jit(solution)/shard_map/psum | solution.py:54
  360.8 1.7 fusion.81
  362.5 2.5 fusion.54
  367.5 6.3 %collective-permute-done.5 = bf16[64,2048]{1,0:T(8,128)(2,1)S(1)} collective-permute-done((bf16[64,2048]{1,0:T(8,128)(2,1)S(1)}, bf16[64,2048]{1,0:T(8,128)(2,1)S(1)}, u32[]{:S(2)}, u32[]{:S(2)}) %collective-permute-start.5) | collective-permute-done | bytes 262176 | tf_op jit(solution)/shard_map/ppermute | solution.py:10
  373.8 1.8 fusion.47
  376.4 1.4 fusion.29
  377.8 32.0 %all-reduce.15.cloned.1.call-done = (f32[64,512]{1,0:T(8,128)}, f32[64,512]{1,0:T(8,128)}) async-done(((f32[64,512]{1,0:T(8,128)}, f32[64,512]{1,0:T(8,128)}), (f32[64,512]{1,0:T(8,128)}, f32[64,512]{1,0:T(8,128)})) %all-reduce.15.cloned.1.call-update) | async-done | bytes 262160 | tf_op jit(solution)/shard_map/psum | solution.py:54
  409.8 1.7 fusion.80
  411.5 2.1 fusion
  413.7 3.4 bitcast_convert_fusion
  417.1 2.3 copy.49
  419.4 2.5 fusion.46
  421.9 23.7 %reduce-scatter.3.cloned.1.call-done = bf16[2048,256]{0,1:T(8,128)(2,1)} async-done(((bf16[2048,512]{0,1:T(8,128)(2,1)}), bf16[2048,256]{0,1:T(8,128)(2,1)}) %reduce-scatter.3.cloned.1.call-update) | async-done | bytes 1048592 | tf_op jit(solution)/shard_map/reduce_scatter | solution.py:79
  445.6 2.3 copy.7
  447.9 32.5 %reduce-scatter.5.cloned.1.call-done = bf16[256,2048]{1,0:T(8,128)(2,1)} async-done(((bf16[512,2048]{1,0:T(8,128)(2,1)}), bf16[256,2048]{1,0:T(8,128)(2,1)}) %reduce-scatter.5.cloned.1.call-update) | async-done | bytes 1048592 | tf_op jit(solution)/shard_map/reduce_scatter | solution.py:82
  (73 shorter events, 27.5 us)
Async XLA Ops:
  7.2 38.2 %copy-start = (bf16[1,4,64,2048]{3,2,1,0:T(8,128)(2,1)S(1)}, bf16[1,4,64,2048]{3,2,1,0:T(8,128)(2,1)}, u32[]{:S(2)}) copy-start(bf16[1,4,64,2048]{3,2,1,0:T(8,128)(2,1)} %param.4) | copy-start | bytes 3145732
  7.2 38.2 %all-gather.7.cloned.1.call-start = ((), (), s32[]{:S(2)}) async-start(), calls=%async_computation.5 | async-start | bytes 3145728 | tf_op jit(solution)/shard_map/all_gather | solution.py:31
  7.9 72.1 %all-gather.5.cloned.1.call-start = ((), (), s32[]{:S(2)}) async-start(), calls=%async_computation.4 | async-start | bytes 3145728 | tf_op jit(solution)/shard_map/all_gather | solution.py:32
  8.7 106.8 %all-reduce.27.cloned.1.call-start = ((), (), s32[]{:S(2)}) async-start(), calls=%async_computation.12 | async-start | bytes 524288 | tf_op jit(solution)/shard_map/psum | solution.py:54
  83.2 34.4 %copy-start.1 = (bf16[1,2048,512]{2,1,0:T(8,128)(2,1)S(1)}, bf16[1,2048,512]{2,1,0:T(8,128)(2,1)}, u32[]{:S(2)}) copy-start(bf16[1,2048,512]{2,1,0:T(8,128)(2,1)} %all-gather.7.cloned.1.call-done) | copy-start | bytes 6291460
  83.2 81.7 %all-reduce.25.cloned.1.call-start = ((), (), s32[]{:S(2)}) async-start(), calls=%async_computation.11 | async-start | bytes 524288 | tf_op jit(solution)/shard_map/psum | solution.py:54
  120.0 11.4 %copy-start.2 = (bf16[1,512,2048]{2,1,0:T(8,128)(2,1)S(1)}, bf16[1,512,2048]{2,1,0:T(8,128)(2,1)}, u32[]{:S(2)}) copy-start(bf16[1,512,2048]{2,1,0:T(8,128)(2,1)} %all-gather.5.cloned.1.call-done) | copy-start | bytes 6291460
  120.0 8.8 %collective-permute-start = (bf16[64,2048]{1,0:T(8,128)(2,1)S(1)}, bf16[64,2048]{1,0:T(8,128)(2,1)S(1)}, u32[]{:S(2)}, u32[]{:S(2)}) collective-permute-start(bf16[64,2048]{1,0:T(8,128)(2,1)S(1)} %get-tuple-element.63), channel_id=1, source_target_pairs={{8,0},{16,8},{24,16},{9,1},{17,9},{25,17},{10,2},{18,10},{26,18},{... | collective-permute-start | bytes 786440 | tf_op jit(solution)/shard_map/ppermute | solution.py:10
  122.6 11.0 %copy-start.15 = (f32[64,512]{1,0:T(8,128)S(1)}, f32[64,512]{1,0:T(8,128)}, u32[]{:S(2)}) copy-start(f32[64,512]{1,0:T(8,128)} %get-tuple-element.19) | copy-start | bytes 393220
  130.7 0.7 copy-start.12
  132.8 81.0 %all-reduce.23.cloned.1.call-start = ((), (), s32[]{:S(2)}) async-start(), calls=%async_computation.10 | async-start | bytes 524288 | tf_op jit(solution)/shard_map/psum | solution.py:54
  169.0 11.4 %copy-start.3 = (bf16[1,512,2048]{2,1,0:T(8,128)(2,1)S(1)}, bf16[1,512,2048]{2,1,0:T(8,128)(2,1)}, u32[]{:S(2)}) copy-start(bf16[1,512,2048]{2,1,0:T(8,128)(2,1)} %all-gather.5.cloned.1.call-done) | copy-start | bytes 6291460
  169.0 8.8 %collective-permute-start.1 = (bf16[64,2048]{1,0:T(8,128)(2,1)S(1)}, bf16[64,2048]{1,0:T(8,128)(2,1)S(1)}, u32[]{:S(2)}, u32[]{:S(2)}) collective-permute-start(bf16[64,2048]{1,0:T(8,128)(2,1)S(1)} %get-tuple-element.55), channel_id=1, source_target_pairs={{8,0},{16,8},{24,16},{9,1},{17,9},{25,17},{10,2},{18,10},{26,18},{... | collective-permute-start | bytes 786440 | tf_op jit(solution)/shard_map/ppermute | solution.py:10
  179.7 0.7 copy-start.11
  181.8 81.0 %all-reduce.21.cloned.1.call-start = ((), (), s32[]{:S(2)}) async-start(), calls=%async_computation.9 | async-start | bytes 524288 | tf_op jit(solution)/shard_map/psum | solution.py:54
  218.0 11.4 %copy-start.4 = (bf16[1,512,2048]{2,1,0:T(8,128)(2,1)S(1)}, bf16[1,512,2048]{2,1,0:T(8,128)(2,1)}, u32[]{:S(2)}) copy-start(bf16[1,512,2048]{2,1,0:T(8,128)(2,1)} %all-gather.5.cloned.1.call-done) | copy-start | bytes 6291460
  218.0 8.8 %collective-permute-start.2 = (bf16[64,2048]{1,0:T(8,128)(2,1)S(1)}, bf16[64,2048]{1,0:T(8,128)(2,1)S(1)}, u32[]{:S(2)}, u32[]{:S(2)}) collective-permute-start(bf16[64,2048]{1,0:T(8,128)(2,1)S(1)} %get-tuple-element.53), channel_id=1, source_target_pairs={{8,0},{16,8},{24,16},{9,1},{17,9},{25,17},{10,2},{18,10},{26,18},{... | collective-permute-start | bytes 786440 | tf_op jit(solution)/shard_map/ppermute | solution.py:10
  228.7 0.7 copy-start.10
  230.8 81.0 %all-reduce.19.cloned.1.call-start = ((), (), s32[]{:S(2)}) async-start(), calls=%async_computation.8 | async-start | bytes 524288 | tf_op jit(solution)/shard_map/psum | solution.py:54
  267.0 11.4 %copy-start.5 = (bf16[1,512,2048]{2,1,0:T(8,128)(2,1)S(1)}, bf16[1,512,2048]{2,1,0:T(8,128)(2,1)}, u32[]{:S(2)}) copy-start(bf16[1,512,2048]{2,1,0:T(8,128)(2,1)} %all-gather.5.cloned.1.call-done) | copy-start | bytes 6291460
  267.0 8.8 %collective-permute-start.3 = (bf16[64,2048]{1,0:T(8,128)(2,1)S(1)}, bf16[64,2048]{1,0:T(8,128)(2,1)S(1)}, u32[]{:S(2)}, u32[]{:S(2)}) collective-permute-start(bf16[64,2048]{1,0:T(8,128)(2,1)S(1)} %get-tuple-element.51), channel_id=1, source_target_pairs={{8,0},{16,8},{24,16},{9,1},{17,9},{25,17},{10,2},{18,10},{26,18},{... | collective-permute-start | bytes 786440 | tf_op jit(solution)/shard_map/ppermute | solution.py:10
  277.7 0.7 copy-start.9
  279.8 81.0 %all-reduce.17.cloned.1.call-start = ((), (), s32[]{:S(2)}) async-start(), calls=%async_computation.7 | async-start | bytes 524288 | tf_op jit(solution)/shard_map/psum | solution.py:54
  316.0 11.4 %copy-start.6 = (bf16[1,512,2048]{2,1,0:T(8,128)(2,1)S(1)}, bf16[1,512,2048]{2,1,0:T(8,128)(2,1)}, u32[]{:S(2)}) copy-start(bf16[1,512,2048]{2,1,0:T(8,128)(2,1)} %all-gather.5.cloned.1.call-done) | copy-start | bytes 6291460
  316.0 8.8 %collective-permute-start.4 = (bf16[64,2048]{1,0:T(8,128)(2,1)S(1)}, bf16[64,2048]{1,0:T(8,128)(2,1)S(1)}, u32[]{:S(2)}, u32[]{:S(2)}) collective-permute-start(bf16[64,2048]{1,0:T(8,128)(2,1)S(1)} %get-tuple-element.49), channel_id=1, source_target_pairs={{8,0},{16,8},{24,16},{9,1},{17,9},{25,17},{10,2},{18,10},{26,18},{... | collective-permute-start | bytes 786440 | tf_op jit(solution)/shard_map/ppermute | solution.py:10
  326.7 0.7 copy-start.8
  328.8 81.0 %all-reduce.15.cloned.1.call-start = ((), (), s32[]{:S(2)}) async-start(), calls=%async_computation.6 | async-start | bytes 524288 | tf_op jit(solution)/shard_map/psum | solution.py:54
  365.0 11.4 %copy-start.7 = (bf16[1,512,2048]{2,1,0:T(8,128)(2,1)S(1)}, bf16[1,512,2048]{2,1,0:T(8,128)(2,1)}, u32[]{:S(2)}) copy-start(bf16[1,512,2048]{2,1,0:T(8,128)(2,1)} %all-gather.5.cloned.1.call-done) | copy-start | bytes 6291460
  365.0 8.8 %collective-permute-start.5 = (bf16[64,2048]{1,0:T(8,128)(2,1)S(1)}, bf16[64,2048]{1,0:T(8,128)(2,1)S(1)}, u32[]{:S(2)}, u32[]{:S(2)}) collective-permute-start(bf16[64,2048]{1,0:T(8,128)(2,1)S(1)} %get-tuple-element.47), channel_id=1, source_target_pairs={{8,0},{16,8},{24,16},{9,1},{17,9},{25,17},{10,2},{18,10},{26,18},{... | collective-permute-start | bytes 786440 | tf_op jit(solution)/shard_map/ppermute | solution.py:10
  375.7 0.7 copy-start.13
  377.8 67.8 %reduce-scatter.3.cloned.1.call-start = ((), (), s32[]{:S(2)}) async-start(), calls=%async_computation.2 | async-start | bytes 3145728 | tf_op jit(solution)/shard_map/reduce_scatter | solution.py:79
  413.6 66.8 %reduce-scatter.5.cloned.1.call-start = ((), (), s32[]{:S(2)}) async-start(), calls=%async_computation.3 | async-start | bytes 3145728 | tf_op jit(solution)/shard_map/reduce_scatter | solution.py:82
  417.1 2.4 copy-start.14
Sparse Core Ops, SparseCore 0:
  9.5 35.7 all-gather.6
  46.9 33.1 all-gather.4
  83.3 32.0 all-reduce.26
  132.9 31.8 all-reduce.24
  181.9 31.8 all-reduce.22
  230.9 31.8 all-reduce.20
  279.9 31.8 all-reduce.18
  328.9 31.8 all-reduce.16
  377.9 31.8 all-reduce.14
  413.7 31.8 reduce-scatter.2
  448.4 31.8 reduce-scatter.4
where the time goes:
time: 488 us; the launch traced here: 487 us
  waiting for transfers between devices  384 us (79%)
  matrix products  44 us (9%)
  other arithmetic  24.4 us (5%)
  between operations  14 us (3%)
  local copies, waits for them, and re-layouts  11.8 us (2%)
  starting transfers between devices  8.92 us (2%)
    psum x7, waiting for transfers between devices, shards(): hidden = lax.psum(hidden_part, 'tensor')  220 us
    ppermute x6, waiting for transfers between devices, shifted(): return lax.ppermute(shard, axis, pairs)  37.7 us
    all_gather x1, waiting for transfers between devices, shards(): lax.all_gather(w_in[0], 'dp', axis=1, tiled=True)  36.6 us
    reduce_scatter x1, waiting for transfers between devices, shards(): lax.psum_scatter(part_out.astype(jnp.bfloat16), 'dp', scatter_dimension=0...  32.5 us
    all_gather x1, waiting for transfers between devices, shards(): lax.all_gather(w_out[0], 'dp', axis=0, tiled=True)  32 us
    select_n x15, other arithmetic, put_slot(): return jnp.where(active, updated, store)  24.4 us
    reduce_scatter x1, waiting for transfers between devices, shards(): lax.psum_scatter(part_in.astype(jnp.bfloat16), 'dp', scatter_dimension=1,...  23.7 us
    dot_general x7, matrix products, shards(): lax.dot_general(dpre, w_in_full, contract, preferred_element_type=jnp.flo...  17.4 us
  transfers between devices with their start and end apart: 17, of which 17 were waited for; matrix products, arithmetic and copies ran while one was open for 5% of the time, Pallas kernels for 0%

commit v1 on v0

--- a/solution.py
+++ b/solution.py
@@ -51,7 +51,7 @@
         hidden_part = lax.dot_general(
             grad_now, w_out_full, contract, preferred_element_type=jnp.float32
         )
-        hidden = lax.psum(hidden_part, "tensor")
+        hidden = jnp.sum(lax.all_gather(hidden_part, "tensor"), axis=0)
         dpre = (hidden * silu_slope(pre_now)).astype(jnp.bfloat16)
         branch = lax.dot_general(dpre, w_in_full, contract, preferred_element_type=jnp.float32)
         back = (grad_now.astype(jnp.float32) + branch).astype(jnp.bfloat16)

time: 488 us -> 366 us (0.75)
  waiting for transfers between devices: 384 us -> 198 us
  blocking collectives: 0 us -> 50.7 us
  other arithmetic: 24.4 us -> 31.5 us
  matrix products: 44 us -> 49.3 us
    psum x7 -> x1, waiting for transfers between devices: 220 us -> 28.3 us  [shards(): pre_now = lax.psum(pre_part, 'tensor')]
    all_gather x0 -> x7, blocking collectives: none -> 50.7 us  [shards(): hidden = jnp.sum(lax.all_gather(hidden_part, 'tensor'), axis=0)]
    ppermute x6, waiting for transfers between devices: 37.7 us -> 51.8 us  [shifted(): return lax.ppermute(shard, axis, pairs)]
    reduce_sum x0 -> x7, other arithmetic: none -> 7.62 us  [shards(): hidden = jnp.sum(lax.all_gather(hidden_part, 'tensor'), axis=0)]
    all_gather x1, waiting for transfers between devices: 32 us -> 25 us  [shards(): lax.all_gather(w_out[0], 'dp', axis=0, tiled=True)]
    dot_general x7, matrix products: 11.6 us -> 16.5 us  [shards(): lax.dot_general(grad_now, w_out_full, contract, preferred_element_type=jn...]
    unnamed x34 -> x28, local copies, waits for them, and re-layouts: 8.85 us -> 10.4 us
  transfers between devices with their start and end apart: 17 -> 11, of which waited for: 17 -> 11; matrix products, arithmetic and copies ran while one was open for 5% -> 7% of each run, Pallas kernels for 0% -> 0%
where the time goes in v1:
time: 366 us; the launch traced here: 364 us
  waiting for transfers between devices  198 us (54%)
  blocking collectives  50.7 us (14%)
  matrix products  49.3 us (13%)
  other arithmetic  31.5 us (9%)
  between operations  14 us (4%)
  local copies, waits for them, and re-layouts  12.6 us (3%)
  starting transfers between devices  8.06 us (2%)
    ppermute x6, waiting for transfers between devices, shifted(): return lax.ppermute(shard, axis, pairs)  51.8 us
    all_gather x7, blocking collectives, shards(): hidden = jnp.sum(lax.all_gather(hidden_part, 'tensor'), axis=0)  50.7 us
    all_gather x1, waiting for transfers between devices, shards(): lax.all_gather(w_in[0], 'dp', axis=1, tiled=True)  36.6 us
    reduce_scatter x1, waiting for transfers between devices, shards(): lax.psum_scatter(part_out.astype(jnp.bfloat16), 'dp', scatter_dimension=0...  32.4 us
    psum x1, waiting for transfers between devices, shards(): pre_now = lax.psum(pre_part, 'tensor')  28.3 us
    all_gather x1, waiting for transfers between devices, shards(): lax.all_gather(w_out[0], 'dp', axis=0, tiled=True)  25 us
    select_n x15, other arithmetic, put_slot(): return jnp.where(active, updated, store)  23.9 us
    reduce_scatter x1, waiting for transfers between devices, shards(): lax.psum_scatter(part_in.astype(jnp.bfloat16), 'dp', scatter_dimension=1,...  22.7 us
  transfers between devices with their start and end apart: 11, of which 11 were waited for; matrix products, arithmetic and copies ran while one was open for 7% of the time, Pallas kernels for 0%

profile of v1, /device:TPU:0, one launch (start us, length us, event | category | flops | bytes accessed | tf_op | source)
XLA Modules:
  0.0 364.5 jit_solution(6873388799679377124)
XLA Ops:
  8.7 36.6 %all-gather.14.cloned.1.call-done = bf16[1,2048,512]{2,1,0:T(8,128)(2,1)} async-done(((bf16[1,2048,256]{2,1,0:T(8,128)(2,1)}), bf16[1,2048,512]{2,1,0:T(8,128)(2,1)}) %all-gather.14.cloned.1.call-update) | async-done | bytes 2097168 | tf_op jit(solution)/shard_map/all_gather | solution.py:31
  45.4 2.9 fusion.27
  55.1 25.0 %all-gather.12.cloned.1.call-done = bf16[1,512,2048]{2,1,0:T(8,128)(2,1)} async-done(((bf16[1,256,2048]{2,1,0:T(8,128)(2,1)}), bf16[1,512,2048]{2,1,0:T(8,128)(2,1)}) %all-gather.12.cloned.1.call-update) | async-done | bytes 2097168 | tf_op jit(solution)/shard_map/all_gather | solution.py:32
  80.1 2.4 fusion.41
  82.5 7.6 %all-gather.1 = f32[256,512]{1,0:T(8,128)} all-gather(f32[64,512]{1,0:T(8,128)S(1)} %fusion.41), channel_id=3, replica_groups=mesh['pipe'=4,'dp'=2,'tensor'=4] {'tensor'}, dimensions={0}, use_global_device_ids=true | all-gather | bytes 655360 | tf_op jit(solution)/shard_map/all_gather | solution.py:54
  91.2 28.3 %all-reduce.3.cloned.1.call-done = (f32[64,512]{1,0:T(8,128)}, f32[64,512]{1,0:T(8,128)}, f32[64,512]{1,0:T(8,128)}, f32[64,512]{1,0:T(8,128)}, f32[64,512]{1,0:...) async-done(((f32[64,512]{1,0:T(8,128)}, f32[64,512]{1,0:T(8,128)}, f32[64,512]{1,0:T(8,128)}, f32[64,512]{1,0:T(8,128)}, f32[64,512]{1,0:T(8,128)}, ...) | async-done | bytes 917520 | tf_op jit(solution)/shard_map/psum | solution.py:50
  121.6 2.5 bitcast_dynamic-update-slice_fusion
  126.5 1.7 select_dynamic-update-slice_fusion
  129.1 4.6 %collective-permute-done = bf16[64,2048]{1,0:T(8,128)(2,1)} collective-permute-done((bf16[64,2048]{1,0:T(8,128)(2,1)}, bf16[64,2048]{1,0:T(8,128)(2,1)}, u32[]{:S(2)}, u32[]{:S(2)}) %collective-permute-start) | collective-permute-done | bytes 262176 | tf_op jit(solution)/shard_map/ppermute | solution.py:10
  133.7 1.9 fusion.52
  136.3 2.3 fusion.39
  138.6 7.6 %all-gather.3 = f32[256,512]{1,0:T(8,128)} all-gather(f32[64,512]{1,0:T(8,128)S(1)} %fusion.39), channel_id=5, replica_groups=mesh['pipe'=4,'dp'=2,'tensor'=4] {'tensor'}, dimensions={0}, use_global_device_ids=true | all-gather | bytes 655360 | tf_op jit(solution)/shard_map/all_gather | solution.py:54
  147.3 1.6 fusion.85
  148.9 2.6 fusion.62
  152.8 9.5 %collective-permute-done.1 = bf16[64,2048]{1,0:T(8,128)(2,1)} collective-permute-done((bf16[64,2048]{1,0:T(8,128)(2,1)}, bf16[64,2048]{1,0:T(8,128)(2,1)}, u32[]{:S(2)}, u32[]{:S(2)}) %collective-permute-start.1) | collective-permute-done | bytes 262176 | tf_op jit(solution)/shard_map/ppermute | solution.py:10
  162.2 1.9 fusion.51
  164.9 2.3 fusion.37
  167.2 7.0 %all-gather.4 = f32[256,512]{1,0:T(8,128)} all-gather(f32[64,512]{1,0:T(8,128)S(1)} %fusion.37), channel_id=6, replica_groups=mesh['pipe'=4,'dp'=2,'tensor'=4] {'tensor'}, dimensions={0}, use_global_device_ids=true | all-gather | bytes 655360 | tf_op jit(solution)/shard_map/all_gather | solution.py:54
  175.3 1.6 fusion.84
  176.9 2.6 fusion.60
  180.7 9.5 %collective-permute-done.2 = bf16[64,2048]{1,0:T(8,128)(2,1)} collective-permute-done((bf16[64,2048]{1,0:T(8,128)(2,1)}, bf16[64,2048]{1,0:T(8,128)(2,1)}, u32[]{:S(2)}, u32[]{:S(2)}) %collective-permute-start.2) | collective-permute-done | bytes 262176 | tf_op jit(solution)/shard_map/ppermute | solution.py:10
  190.2 1.9 fusion.50
  192.8 2.3 fusion.35
  195.2 7.3 %all-gather.5 = f32[256,512]{1,0:T(8,128)} all-gather(f32[64,512]{1,0:T(8,128)S(1)} %fusion.35), channel_id=7, replica_groups=mesh['pipe'=4,'dp'=2,'tensor'=4] {'tensor'}, dimensions={0}, use_global_device_ids=true | all-gather | bytes 655360 | tf_op jit(solution)/shard_map/all_gather | solution.py:54
  205.2 2.6 fusion.58
  209.1 9.5 %collective-permute-done.3 = bf16[64,2048]{1,0:T(8,128)(2,1)} collective-permute-done((bf16[64,2048]{1,0:T(8,128)(2,1)}, bf16[64,2048]{1,0:T(8,128)(2,1)}, u32[]{:S(2)}, u32[]{:S(2)}) %collective-permute-start.3) | collective-permute-done | bytes 262176 | tf_op jit(solution)/shard_map/ppermute | solution.py:10
  218.5 1.9 fusion.49
  221.2 2.3 fusion.33
  223.5 7.0 %all-gather.6 = f32[256,512]{1,0:T(8,128)} all-gather(f32[64,512]{1,0:T(8,128)S(1)} %fusion.33), channel_id=8, replica_groups=mesh['pipe'=4,'dp'=2,'tensor'=4] {'tensor'}, dimensions={0}, use_global_device_ids=true | all-gather | bytes 655360 | tf_op jit(solution)/shard_map/all_gather | solution.py:54
  233.2 2.6 fusion.56
  237.0 9.5 %collective-permute-done.4 = bf16[64,2048]{1,0:T(8,128)(2,1)} collective-permute-done((bf16[64,2048]{1,0:T(8,128)(2,1)}, bf16[64,2048]{1,0:T(8,128)(2,1)}, u32[]{:S(2)}, u32[]{:S(2)}) %collective-permute-start.4) | collective-permute-done | bytes 262176 | tf_op jit(solution)/shard_map/ppermute | solution.py:10
  246.5 1.9 fusion.48
  249.1 2.3 fusion.31
  251.5 7.3 %all-gather.7 = f32[256,512]{1,0:T(8,128)} all-gather(f32[64,512]{1,0:T(8,128)S(1)} %fusion.31), channel_id=9, replica_groups=mesh['pipe'=4,'dp'=2,'tensor'=4] {'tensor'}, dimensions={0}, use_global_device_ids=true | all-gather | bytes 655360 | tf_op jit(solution)/shard_map/all_gather | solution.py:54
  259.9 1.6 fusion.81
  261.5 2.6 fusion.54
  265.6 9.3 %collective-permute-done.5 = bf16[64,2048]{1,0:T(8,128)(2,1)} collective-permute-done((bf16[64,2048]{1,0:T(8,128)(2,1)}, bf16[64,2048]{1,0:T(8,128)(2,1)}, u32[]{:S(2)}, u32[]{:S(2)}) %collective-permute-start.5) | collective-permute-done | bytes 262176 | tf_op jit(solution)/shard_map/ppermute | solution.py:10
  274.9 1.9 fusion.47
  277.5 2.3 fusion.29
  279.8 7.0 %all-gather.8 = f32[256,512]{1,0:T(8,128)} all-gather(f32[64,512]{1,0:T(8,128)S(1)} %fusion.29), channel_id=10, replica_groups=mesh['pipe'=4,'dp'=2,'tensor'=4] {'tensor'}, dimensions={0}, use_global_device_ids=true | all-gather | bytes 655360 | tf_op jit(solution)/shard_map/all_gather | solution.py:54
  287.9 1.6 fusion.80
  289.5 2.1 fusion
  292.5 3.3 bitcast_convert_fusion
  295.8 2.3 copy.42
  298.2 2.4 fusion.46
  300.6 22.7 %reduce-scatter.3.cloned.1.call-done = bf16[2048,256]{0,1:T(8,128)(2,1)} async-done(((bf16[2048,512]{0,1:T(8,128)(2,1)}), bf16[2048,256]{0,1:T(8,128)(2,1)}) %reduce-scatter.3.cloned.1.call-update) | async-done | bytes 1048592 | tf_op jit(solution)/shard_map/reduce_scatter | solution.py:79
  323.3 2.3 copy.7
  325.6 32.4 %reduce-scatter.5.cloned.1.call-done = bf16[256,2048]{1,0:T(8,128)(2,1)} async-done(((bf16[512,2048]{1,0:T(8,128)(2,1)}), bf16[256,2048]{1,0:T(8,128)(2,1)}) %reduce-scatter.5.cloned.1.call-update) | async-done | bytes 1048592 | tf_op jit(solution)/shard_map/reduce_scatter | solution.py:82
  (63 shorter events, 36.1 us)
Async XLA Ops:
  7.2 38.2 %copy-start = (bf16[1,4,64,2048]{3,2,1,0:T(8,128)(2,1)S(1)}, bf16[1,4,64,2048]{3,2,1,0:T(8,128)(2,1)}, u32[]{:S(2)}) copy-start(bf16[1,4,64,2048]{3,2,1,0:T(8,128)(2,1)} %param.4) | copy-start | bytes 3145732
  7.2 38.2 %all-gather.14.cloned.1.call-start = ((), (), s32[]{:S(2)}) async-start(), calls=%async_computation.5 | async-start | bytes 3145728 | tf_op jit(solution)/shard_map/all_gather | solution.py:31
  7.9 72.1 %all-gather.12.cloned.1.call-start = ((), (), s32[]{:S(2)}) async-start(), calls=%async_computation.4 | async-start | bytes 3145728 | tf_op jit(solution)/shard_map/all_gather | solution.py:32
  8.7 110.9 %all-reduce.3.cloned.1.call-start = ((), (), s32[]{:S(2)}) async-start(), calls=%async_computation.6 | async-start | bytes 1835008 | tf_op jit(solution)/shard_map/psum | solution.py:50
  45.4 2.9 copy-start.1
  55.0 268.3 %reduce-scatter.3.cloned.1.call-start = ((), (), s32[]{:S(2)}) async-start(), calls=%async_computation.2 | async-start | bytes 3145728 | tf_op jit(solution)/shard_map/reduce_scatter | solution.py:79
  121.6 6.7 %copy-start.11 = (f32[64,512]{1,0:T(8,128)S(1)}, f32[64,512]{1,0:T(8,128)}, u32[]{:S(2)}) copy-start(f32[64,512]{1,0:T(8,128)} %get-tuple-element.6) | copy-start | bytes 393220
  124.1 9.5 %collective-permute-start = (bf16[64,2048]{1,0:T(8,128)(2,1)}, bf16[64,2048]{1,0:T(8,128)(2,1)}, u32[]{:S(2)}, u32[]{:S(2)}) collective-permute-start(bf16[64,2048]{1,0:T(8,128)(2,1)} %get-tuple-element.56), channel_id=1, source_target_pairs={{8,0},{16,8},{24,16},{9,1},{17,9},{25,17},{10,2},{18,10},{26,18},{... | collective-permute-start | bytes 786440 | tf_op jit(solution)/shard_map/ppermute | solution.py:10
  128.3 0.7 copy-start.9
  135.6 0.7 copy-start.2
  151.5 10.8 %collective-permute-start.1 = (bf16[64,2048]{1,0:T(8,128)(2,1)}, bf16[64,2048]{1,0:T(8,128)(2,1)}, u32[]{:S(2)}, u32[]{:S(2)}) collective-permute-start(bf16[64,2048]{1,0:T(8,128)(2,1)} %get-tuple-element.48), channel_id=1, source_target_pairs={{8,0},{16,8},{24,16},{9,1},{17,9},{25,17},{10,2},{18,10},{26,18},{... | collective-permute-start | bytes 786440 | tf_op jit(solution)/shard_map/ppermute | solution.py:10
  164.2 0.7 copy-start.3
  179.5 10.8 %collective-permute-start.2 = (bf16[64,2048]{1,0:T(8,128)(2,1)}, bf16[64,2048]{1,0:T(8,128)(2,1)}, u32[]{:S(2)}, u32[]{:S(2)}) collective-permute-start(bf16[64,2048]{1,0:T(8,128)(2,1)} %get-tuple-element.46), channel_id=1, source_target_pairs={{8,0},{16,8},{24,16},{9,1},{17,9},{25,17},{10,2},{18,10},{26,18},{... | collective-permute-start | bytes 786440 | tf_op jit(solution)/shard_map/ppermute | solution.py:10
  192.1 0.7 copy-start.4
  207.8 10.8 %collective-permute-start.3 = (bf16[64,2048]{1,0:T(8,128)(2,1)}, bf16[64,2048]{1,0:T(8,128)(2,1)}, u32[]{:S(2)}, u32[]{:S(2)}) collective-permute-start(bf16[64,2048]{1,0:T(8,128)(2,1)} %get-tuple-element.44), channel_id=1, source_target_pairs={{8,0},{16,8},{24,16},{9,1},{17,9},{25,17},{10,2},{18,10},{26,18},{... | collective-permute-start | bytes 786440 | tf_op jit(solution)/shard_map/ppermute | solution.py:10
  220.5 0.7 copy-start.5
  235.8 10.8 %collective-permute-start.4 = (bf16[64,2048]{1,0:T(8,128)(2,1)}, bf16[64,2048]{1,0:T(8,128)(2,1)}, u32[]{:S(2)}, u32[]{:S(2)}) collective-permute-start(bf16[64,2048]{1,0:T(8,128)(2,1)} %get-tuple-element.42), channel_id=1, source_target_pairs={{8,0},{16,8},{24,16},{9,1},{17,9},{25,17},{10,2},{18,10},{26,18},{... | collective-permute-start | bytes 786440 | tf_op jit(solution)/shard_map/ppermute | solution.py:10
  248.4 0.7 copy-start.6
  264.1 10.8 %collective-permute-start.5 = (bf16[64,2048]{1,0:T(8,128)(2,1)}, bf16[64,2048]{1,0:T(8,128)(2,1)}, u32[]{:S(2)}, u32[]{:S(2)}) collective-permute-start(bf16[64,2048]{1,0:T(8,128)(2,1)} %get-tuple-element.40), channel_id=1, source_target_pairs={{8,0},{16,8},{24,16},{9,1},{17,9},{25,17},{10,2},{18,10},{26,18},{... | collective-permute-start | bytes 786440 | tf_op jit(solution)/shard_map/ppermute | solution.py:10
  276.8 0.7 copy-start.7
  291.6 0.9 copy-start.10
  291.6 66.3 %reduce-scatter.5.cloned.1.call-start = ((), (), s32[]{:S(2)}) async-start(), calls=%async_computation.3 | async-start | bytes 3145728 | tf_op jit(solution)/shard_map/reduce_scatter | solution.py:82
  295.8 2.4 copy-start.8
  295.8 2.4 copy-start.12
Sparse Core Ops, SparseCore 0:
  9.5 35.7 all-gather.13
  46.9 33.1 all-gather.11
  83.5 35.9 all-reduce.2
  291.7 31.5 reduce-scatter.2
  326.1 31.8 reduce-scatter.4
